TPU v7x, 32 devices: a whole 2x2x4 slice. The times are simulated.
32 devices in a mesh: row: 4 (over z), col: 8 (over y, x, core).
Axes of the slice: x: 2, y: 2, z: 4, core: 2. Of those that a mesh axis runs over, the one named last changes fastest.
Arguments:
- pair: bfloat16 [256, 256, 128], P('row', 'col'), may hold values from -6 to 6
- residue_mask: int32 [256], replicated, may hold values 0 or 1
- norm_gain: float32 [2, 2, 128], replicated, may hold values from 0.25 to 1.75
- norm_bias: float32 [2, 2, 128], replicated, may hold values from -3 to 3
- w_in_q: bfloat16 [2, 128, 640], replicated, may hold values from -0.5 to 0.5
- exp_in: int32 [2, 4, 20], replicated, may hold values from -2 to 1
- w_out_q: bfloat16 [2, 128, 128], replicated, may hold values from -0.5 to 0.5
- exp_out: int32 [2, 4, 4], replicated, may hold values from -2 to 1
Outputs:
- pair_out: bfloat16 [256, 256, 128], P('row', 'col')
All inputs are finite; a program needn't handle non-finite values.
Results may differ from a plain program's by a relative error of at most 0.0056.
Values may be sent and summed in bfloat16 or wider, within the bound.
No kernel may reach another device: no remote copies, remote signals or barrier semaphores. Data moves between devices by JAX's collectives and lax.ppermute only.
A program may use at most 128 MiB of HBM per device.

v0:
```python
import jax
import jax.numpy as jnp
from jax import lax
from jax.sharding import PartitionSpec as P

BLK = 32


def spread(x, axis, root):
    mine = lax.axis_index(axis) == root
    return lax.psum(jnp.where(mine, x, jnp.zeros_like(x)), axis)


def layer_norm(values, scale_vec, shift_vec):
    average = jnp.mean(values, axis=-1, keepdims=True)
    centred = values - average
    variance = jnp.mean(centred * centred, axis=-1, keepdims=True)
    return centred * lax.rsqrt(variance + 1e-05) * scale_vec + shift_vec


def dequantize(quantized, exponents, block_size):
    scales = jnp.exp2(exponents.astype(jnp.float32))
    scales = jnp.repeat(jnp.repeat(scales, block_size, axis=0), block_size, axis=1)
    return (quantized.astype(jnp.float32) * scales).astype(jnp.bfloat16)


def project(pair_in, row_mask, col_mask, layer, norm_gain, norm_bias, w_in_q, exp_in):
    rows_n, cols_n, width = pair_in.shape
    normed = layer_norm(
        pair_in.astype(jnp.float32), norm_gain[layer, 0], norm_bias[layer, 0]
    ).astype(jnp.bfloat16)
    weights_in = dequantize(w_in_q[layer], exp_in[layer], BLK)
    projected = jnp.dot(
        normed.reshape(rows_n * cols_n, width), weights_in, preferred_element_type=jnp.float32
    )
    projected = projected.reshape(rows_n, cols_n, 5 * width)
    pair_mask = (row_mask[:, None] * col_mask[None, :])[:, :, None]
    left = (
        jax.nn.sigmoid(projected[:, :, 0:width]) * projected[:, :, width : 2 * width] * pair_mask
    ).astype(jnp.bfloat16)
    right = (
        jax.nn.sigmoid(projected[:, :, 2 * width : 3 * width])
        * projected[:, :, 3 * width : 4 * width]
        * pair_mask
    ).astype(jnp.bfloat16)
    gate = jax.nn.sigmoid(projected[:, :, 4 * width :])
    return (left, right, gate)


def finish(pair_in, summed, gate, layer, norm_gain, norm_bias, w_out_q, exp_out):
    rows_n, cols_n, width = pair_in.shape
    normed = layer_norm(summed, norm_gain[layer, 1], norm_bias[layer, 1]).astype(jnp.bfloat16)
    weights_out = dequantize(w_out_q[layer], exp_out[layer], BLK)
    update = jnp.dot(
        normed.reshape(rows_n * cols_n, width), weights_out, preferred_element_type=jnp.float32
    )
    update = update.reshape(rows_n, cols_n, width)
    return (pair_in.astype(jnp.float32) + gate * update).astype(jnp.bfloat16)


def shards(pair, residue_mask, norm_gain, norm_bias, w_in_q, exp_in, w_out_q, exp_out):
    rows_n, cols_n, width = pair.shape
    row_count = lax.axis_size("row")
    col_count = lax.axis_size("col")
    col_ratio = col_count // row_count
    row_place = lax.axis_index("row")
    col_place = lax.axis_index("col")
    mask_all = residue_mask.astype(jnp.float32)
    row_mask = lax.dynamic_slice_in_dim(mask_all, row_place * rows_n, rows_n)
    col_mask = lax.dynamic_slice_in_dim(mask_all, col_place * cols_n, cols_n)
    left, right, gate = project(pair, row_mask, col_mask, 0, norm_gain, norm_bias, w_in_q, exp_in)
    right_panel = lax.all_gather(right, "col", axis=1, tiled=True)
    chosen = lax.dynamic_slice_in_dim(right_panel, col_place % col_ratio * cols_n, cols_n, 0)
    right_rows = spread(chosen, "row", col_place // col_ratio)
    selected = right_rows
    summed = jnp.einsum(
        "ikc,jkc->ijc",
        lax.all_gather(left, "col", axis=1, tiled=True),
        selected,
        preferred_element_type=jnp.float32,
    )
    pair_mid = finish(pair, summed, gate, 0, norm_gain, norm_bias, w_out_q, exp_out)
    left, right, gate = project(
        pair_mid, row_mask, col_mask, 1, norm_gain, norm_bias, w_in_q, exp_in
    )
    column_panel = lax.all_gather(left, "row", axis=0, tiled=True)
    pieces_list = []
    for offset_idx in range(col_ratio):
        pieces_list.append(spread(column_panel, "col", row_place * col_ratio + offset_idx))
    left_cols = jnp.concatenate(pieces_list, axis=1)
    selected = left_cols
    summed = jnp.einsum(
        "kic,kjc->ijc",
        selected,
        lax.all_gather(right, "row", axis=0, tiled=True),
        preferred_element_type=jnp.float32,
    )
    return finish(pair_mid, summed, gate, 1, norm_gain, norm_bias, w_out_q, exp_out)


def solution(mesh):
    placed = (P("row", "col", None), P(), P(), P(), P(), P(), P(), P())
    return jax.shard_map(
        shards, mesh=mesh, in_specs=placed, out_specs=P("row", "col", None), check_vma=False
    )
```

profile of v0, /device:TPU:0, one launch (start us, length us, event | category | flops | bytes accessed | tf_op | source)
XLA Modules:
  0.0 389.6 jit_solution(5334776976437683013)
XLA Ops:
  6.5 0.7 convert_element_type.115
  7.3 0.1 dynamic_slice.10
  7.4 0.1 dynamic_slice.9
  7.4 1.0 fusion.65
  8.5 0.2 copy.126
  8.6 0.7 exponential_bitcast_fusion.1
  9.3 0.1 copy.96
  9.4 0.1 broadcast_in_dim.49
  9.5 0.1 reshape.147
  9.6 1.4 convert_reduce_fusion.1
  11.0 0.1 copy.91
  11.1 0.1 copy.92
  11.2 0.6 fusion.14
  11.8 0.1 copy.93
  11.9 0.1 copy.94
  12.0 0.1 broadcast_multiply_fusion
  12.1 1.0 fusion.44
  13.2 2.1 fusion.32
  15.2 0.6 copy-done
  15.9 0.7 all-gather.7.cloned.1.call-update
  16.7 39.4 %all-gather.5.cloned.1.call-done = bf16[64,256,128]{2,1,0:T(8,128)(2,1)} async-done(((bf16[64,32,128]{2,1,0:T(8,128)(2,1)}), bf16[64,256,128]{2,1,0:T(8,128)(2,1)}) %all-gather.5.cloned.1.call-update) | async-done | bytes 4194320 | tf_op jit(solution)/shard_map/all_gather | solution.py:72
  56.1 3.1 dynamic-slice_select_fusion
  59.3 0.8 copy-done.3
  60.0 0.1 copy.127
  60.2 0.1 copy.101
  60.3 0.1 broadcast_in_dim.53
  60.3 0.1 reshape.148
  60.4 0.2 copy.128
  60.6 0.1 copy.109
  60.7 0.1 broadcast_in_dim.56
  60.8 0.1 reshape.149
  60.9 34.4 %all-gather.7.cloned.1.call-done = bf16[64,256,128]{2,1,0:T(8,128)(2,1)} async-done(((bf16[64,32,128]{2,1,0:T(8,128)(2,1)}), bf16[64,256,128]{2,1,0:T(8,128)(2,1)}) %all-gather.7.cloned.1.call-update) | async-done | bytes 4194320 | tf_op jit(solution)/shard_map/all_gather | solution.py:78
  95.4 15.6 %copy.99 = bf16[64,256,128]{0,1,2:T(8,128)(2,1)} copy(bf16[64,256,128]{2,1,0:T(8,128)(2,1)} %all-gather.7.cloned.1.call-done) | data formatting | bytes 8388608 | tf_op jit(solution)/shard_map/all_gather | solution.py:78
  111.0 72.9 %all-reduce.4.cloned.1.call-done = bf16[32,256,128]{2,1,0:T(8,128)(2,1)} async-done(((bf16[32,256,128]{2,1,0:T(8,128)(2,1)}), bf16[32,256,128]{2,1,0:T(8,128)(2,1)}) %all-reduce.4.cloned.1.call-update) | async-done | bytes 2097168 | tf_op jit(solution)/shard_map/psum | solution.py:11
  183.9 3.4 copy.98
  187.3 4.8 %bitcast_reduce_fusion.1 = (f32[64,32]{0,1:T(8,128)S(1)}, f32[128,32,64]{2,1,0:T(8,128)S(1)}) fusion(bf16[32,256,128]{1,0,2:T(8,128)(2,1)S(1)} %copy.98, bf16[64,256,128]{0,1,2:T(8,128)(2,1)} %copy.99), kind=kOutput, calls=%fused_computation.7 | convolution fusion | flops 134477824 | bytes 7348224 | tf_op jit(solution)/shard_map/ikc,jkc->ijc/dot_general | solution.py:76
  192.1 0.3 multiply_reduce_fusion.1
  192.5 0.4 add_convert_fusion.1
  192.9 1.5 copy.102
  194.5 1.8 convert_reduce_fusion
  196.3 0.1 copy.105
  196.4 0.6 fusion.10
  197.0 0.1 copy.106
  197.1 0.1 copy.107
  197.2 1.0 fusion.46
  198.3 2.0 fusion.19
  200.2 0.7 copy-done.1
  201.0 0.5 all-gather.9.cloned.1.call-update
  201.5 0.2 all-reduce.6.cloned.1.call-start
  201.7 44.0 %all-gather.11.cloned.1.call-done = bf16[256,32,128]{2,1,0:T(8,128)(2,1)} async-done(((bf16[64,32,128]{2,1,0:T(8,128)(2,1)}), bf16[256,32,128]{2,1,0:T(8,128)(2,1)}) %all-gather.11.cloned.1.call-update) | async-done | bytes 2097168 | tf_op jit(solution)/shard_map/all_gather | solution.py:86
  245.8 3.9 %copy.111 = bf16[256,32,128]{0,1,2:T(8,128)(2,1)S(1)} copy(bf16[256,32,128]{2,1,0:T(8,128)(2,1)} %all-gather.11.cloned.1.call-done) | data formatting | bytes 4194304 | tf_op jit(solution)/shard_map/all_gather | solution.py:86
  249.7 2.3 broadcast_select_fusion.1
  252.0 0.1 copy.129
  252.1 0.1 copy.115
  252.2 0.1 broadcast_in_dim.59
  252.3 0.1 reshape.150
  252.4 39.3 %all-gather.9.cloned.1.call-done = bf16[256,32,128]{2,1,0:T(8,128)(2,1)} async-done(((bf16[64,32,128]{2,1,0:T(8,128)(2,1)}), bf16[256,32,128]{2,1,0:T(8,128)(2,1)}) %all-gather.9.cloned.1.call-update) | async-done | bytes 2097168 | tf_op jit(solution)/shard_map/all_gather | solution.py:95
  291.7 3.9 %copy.113 = bf16[256,32,128]{0,1,2:T(8,128)(2,1)S(1)} copy(bf16[256,32,128]{2,1,0:T(8,128)(2,1)} %all-gather.9.cloned.1.call-done) | data formatting | bytes 4194304 | tf_op jit(solution)/shard_map/all_gather | solution.py:95
  295.6 78.9 %all-reduce.6.cloned.1.call-done = (bf16[256,32,128]{0,1,2:T(8,128)(2,1)}, bf16[256,32,128]{0,1,2:T(8,128)(2,1)}) async-done(((bf16[256,32,128]{0,1,2:T(8,128)(2,1)}, bf16[256,32,128]{0,1,2:T(8,128)(2,1)}), (bf16[256,32,128]{0,1,2:T(8,128)(2,1)}, bf16[256,32,128]{0,1,2:T(8,128)(2,1)})) %all-reduce.6.cloned.1.call-update) | async-done | bytes 4194320 | tf_op jit(solution)/shard_map/psum | solution.py:11
  374.5 3.4 bitcast_reduce_fusion
  378.0 0.3 multiply_reduce_fusion
  378.3 0.4 add_convert_fusion
  378.7 1.5 copy.116
  380.3 2.4 fusion.5
  (36 shorter events, 0.5 us)
Async XLA Ops:
  6.5 4.6 %copy-start.2 = (bf16[64,32,128]{2,1,0:T(8,128)(2,1)S(1)}, bf16[64,32,128]{2,1,0:T(8,128)(2,1)}, u32[]{:S(2)}) copy-start(bf16[64,32,128]{2,1,0:T(8,128)(2,1)} %param.8) | copy-start | bytes 1572868
  6.5 5.5 %copy-start.6 = (f32[2,2,128]{2,1,0:T(2,128)S(1)}, f32[2,2,128]{2,1,0:T(2,128)}, u32[]{:S(2)}) copy-start(f32[2,2,128]{2,1,0:T(2,128)} %param.10) | copy-start | bytes 6148
  6.5 5.5 %copy-start.5 = (f32[2,2,128]{2,1,0:T(2,128)S(1)}, f32[2,2,128]{2,1,0:T(2,128)}, u32[]{:S(2)}) copy-start(f32[2,2,128]{2,1,0:T(2,128)} %param.11) | copy-start | bytes 6148
  6.5 49.6 %all-gather.5.cloned.1.call-start = ((), (), s32[]{:S(2)}) async-start(), calls=%async_computation | async-start | bytes 4718592 | tf_op jit(solution)/shard_map/all_gather | solution.py:72
  13.2 2.7 copy-start
  15.9 79.5 %all-gather.7.cloned.1.call-start = ((), (), s32[]{:S(2)}) async-start(), calls=%async_computation.2 | async-start | bytes 4718592 | tf_op jit(solution)/shard_map/all_gather | solution.py:78
  16.7 167.3 %all-reduce.4.cloned.1.call-start = ((), (), s32[]{:S(2)}) async-start(), calls=%async_computation.1 | async-start | bytes 4194304 | tf_op jit(solution)/shard_map/psum | solution.py:11
  59.2 0.8 copy-start.3
  59.2 1.0 copy-start.4
  59.2 186.6 %all-gather.11.cloned.1.call-start = ((), (), s32[]{:S(2)}) async-start(), calls=%async_computation.4 | async-start | bytes 2621440 | tf_op jit(solution)/shard_map/all_gather | solution.py:86
  198.2 2.6 copy-start.1
  200.9 90.8 %all-gather.9.cloned.1.call-start = ((), (), s32[]{:S(2)}) async-start(), calls=%async_computation.3 | async-start | bytes 2621440 | tf_op jit(solution)/shard_map/all_gather | solution.py:95
  201.5 173.0 %all-reduce.6.cloned.1.call-start = ((), (), s32[]{:S(2)}) async-start(), calls=%async_computation.5 | async-start | bytes 8388608 | tf_op jit(solution)/shard_map/psum | solution.py:11
Sparse Core Ops, SparseCore 0:
  16.0 40.0 all-gather.4
  58.0 37.3 all-gather.6
  97.7 86.1 all-reduce.3
  201.0 44.6 all-gather.10
  247.2 44.4 all-gather.8
  294.8 79.6 all-reduce.5
where the time goes:
time: 390 us
  waiting for transfers between devices  310 us (79%)
  local copies, waits for them, and re-layouts  35.4 us (9%)
  other arithmetic  15.3 us (4%)
  matrix products  14.5 us (4%)
  between operations  13.8 us (4%)
    psum x2, waiting for transfers between devices, spread(): return lax.psum(jnp.where(mine, x, jnp.zeros_like(x)), axis)  152 us
    all_gather x1, waiting for transfers between devices, shards(): column_panel = lax.all_gather(left, 'row', axis=0, tiled=True)  44 us
    all_gather x1, waiting for transfers between devices, shards(): right_panel = lax.all_gather(right, 'col', axis=1, tiled=True)  39.4 us
    all_gather x1, waiting for transfers between devices, shards(): lax.all_gather(right, 'row', axis=0, tiled=True)  39.3 us
    all_gather x1, waiting for transfers between devices, shards(): lax.all_gather(left, 'col', axis=1, tiled=True)  34.4 us
    all_gather x1, local copies, waits for them, and re-layouts, shards(): lax.all_gather(left, 'col', axis=1, tiled=True)  15.6 us
  transfers between devices with their start and end apart: 6, of which 6 were waited for; matrix products, arithmetic and copies ran while one was open for 8% of the time, Pallas kernels for 0%

commit v1 on v0

--- a/solution.py
+++ b/solution.py
@@ -4,6 +4,32 @@
 from jax.sharding import PartitionSpec as P
 
 BLK = 32
+
+
+def ways_mix(block_here, d_out):
+    new = list(block_here.shape[1:])
+    new[d_out] *= block_here.shape[0]
+    block_next = jnp.moveaxis(block_here, 0, d_out).reshape(new)
+    return block_next
+
+
+def report_lines_for(local_x, axis_name):
+    n_blocks = lax.axis_size(axis_name)
+    u_next = local_x[None]
+    for src_i in range(n_blocks.bit_length() - 1):
+        z2 = 1 << src_i
+        met_up = lax.ppermute(
+            u_next, axis_name=axis_name, perm=tuple(((k, k ^ z2) for k in range(n_blocks)))
+        )
+        step_out = jnp.stack([u_next, met_up])
+        known = lax.axis_index(axis_name) >> src_i & 1
+        u_next = jnp.where(known == 0, step_out, step_out[::-1]).reshape(-1, *local_x.shape)
+    return u_next
+
+
+def _set_sides(row_data, t0, on_dim):
+    piece_next = ways_mix(report_lines_for(row_data, t0), on_dim)
+    return piece_next
 
 
 def spread(x, axis, root):
@@ -90,10 +116,7 @@
     left_cols = jnp.concatenate(pieces_list, axis=1)
     selected = left_cols
     summed = jnp.einsum(
-        "kic,kjc->ijc",
-        selected,
-        lax.all_gather(right, "row", axis=0, tiled=True),
-        preferred_element_type=jnp.float32,
+        "kic,kjc->ijc", selected, _set_sides(right, "row", 0), preferred_element_type=jnp.float32
     )
     return finish(pair_mid, summed, gate, 1, norm_gain, norm_bias, w_out_q, exp_out)
 

time: 390 us -> 351 us (0.900)
  waiting for transfers between devices: 310 us -> 265 us
    psum x2, waiting for transfers between devices: 152 us -> 98 us  [spread(): return lax.psum(jnp.where(mine, x, jnp.zeros_like(x)), axis)]
    ppermute x0 -> x2, waiting for transfers between devices: none -> 45.9 us  [report_lines_for(): lax.ppermute(u_next, axis_name=axis_name, perm=tuple(((k, k ^ z2) for k i...]
    all_gather x1 -> x0, waiting for transfers between devices: 39.3 us -> none  [shards(): lax.all_gather(right, 'row', axis=0, tiled=True)]
    all_gather x1 -> x0, local copies, waits for them, and re-layouts: 3.91 us -> none  [shards(): lax.all_gather(right, 'row', axis=0, tiled=True)]
  transfers between devices with their start and end apart: 6 -> 7, of which waited for: 6 -> 6; matrix products, arithmetic and copies ran while one was open for 8% -> 9% of each run, Pallas kernels for 0% -> 0%
where the time goes in v1:
time: 351 us
  waiting for transfers between devices  265 us (75%)
  local copies, waits for them, and re-layouts  35 us (10%)
  other arithmetic  18.6 us (5%)
  matrix products  15.1 us (4%)
  between operations  13.5 us (4%)
    psum x2, waiting for transfers between devices, spread(): return lax.psum(jnp.where(mine, x, jnp.zeros_like(x)), axis)  98 us
    all_gather x1, waiting for transfers between devices, shards(): column_panel = lax.all_gather(left, 'row', axis=0, tiled=True)  47 us
    ppermute x2, waiting for transfers between devices, report_lines_for(): lax.ppermute(u_next, axis_name=axis_name, perm=tuple(((k, k ^ z2) for k i...  45.9 us
    all_gather x1, waiting for transfers between devices, shards(): right_panel = lax.all_gather(right, 'col', axis=1, tiled=True)  39.4 us
    all_gather x1, waiting for transfers between devices, shards(): lax.all_gather(left, 'col', axis=1, tiled=True)  34.4 us
    all_gather x1, local copies, waits for them, and re-layouts, shards(): lax.all_gather(left, 'col', axis=1, tiled=True)  15.6 us
  transfers between devices with their start and end apart: 7, of which 6 were waited for; matrix products, arithmetic and copies ran while one was open for 9% of the time, Pallas kernels for 0%

profile of v1, /device:TPU:0, one launch (start us, length us, event | category | flops | bytes accessed | tf_op | source)
XLA Modules:
  0.0 350.6 jit_solution(12621617376877053779)
XLA Ops:
  6.5 0.7 convert_element_type.115
  7.3 0.1 dynamic_slice.10
  7.4 0.1 dynamic_slice.9
  7.4 1.0 fusion.67
  8.5 0.2 copy.126
  8.6 0.7 exponential_bitcast_fusion.1
  9.3 0.1 copy.96
  9.4 0.1 broadcast_in_dim.52
  9.5 0.1 reshape.150
  9.6 1.4 convert_reduce_fusion.1
  11.1 0.1 copy.92
  11.2 0.6 fusion.14
  11.9 0.1 copy.94
  12.0 0.1 broadcast_multiply_fusion
  12.1 1.0 fusion.46
  13.2 2.1 fusion.32
  15.3 0.6 copy-done
  15.9 0.7 all-gather.6.cloned.1.call-update
  16.7 39.4 %all-gather.4.cloned.1.call-done = bf16[64,256,128]{2,1,0:T(8,128)(2,1)} async-done(((bf16[64,32,128]{2,1,0:T(8,128)(2,1)}), bf16[64,256,128]{2,1,0:T(8,128)(2,1)}) %all-gather.4.cloned.1.call-update) | async-done | bytes 4194320 | tf_op jit(solution)/shard_map/all_gather | solution.py:98
  56.1 3.1 dynamic-slice_select_fusion
  59.2 0.8 copy-done.3
  60.0 0.1 copy.127
  60.1 0.1 copy.101
  60.3 0.1 reshape.151
  60.4 0.2 copy.128
  60.6 0.1 copy.109
  60.7 0.1 broadcast_in_dim.59
  60.8 0.1 reshape.152
  60.9 34.4 %all-gather.6.cloned.1.call-done = bf16[64,256,128]{2,1,0:T(8,128)(2,1)} async-done(((bf16[64,32,128]{2,1,0:T(8,128)(2,1)}), bf16[64,256,128]{2,1,0:T(8,128)(2,1)}) %all-gather.6.cloned.1.call-update) | async-done | bytes 4194320 | tf_op jit(solution)/shard_map/all_gather | solution.py:104
  95.4 15.6 %copy.99 = bf16[64,256,128]{0,1,2:T(8,128)(2,1)} copy(bf16[64,256,128]{2,1,0:T(8,128)(2,1)} %all-gather.6.cloned.1.call-done) | data formatting | bytes 8388608 | tf_op jit(solution)/shard_map/all_gather | solution.py:104
  111.0 72.9 %all-reduce.4.cloned.1.call-done = bf16[32,256,128]{2,1,0:T(8,128)(2,1)} async-done(((bf16[32,256,128]{2,1,0:T(8,128)(2,1)}), bf16[32,256,128]{2,1,0:T(8,128)(2,1)}) %all-reduce.4.cloned.1.call-update) | async-done | bytes 2097168 | tf_op jit(solution)/shard_map/psum | solution.py:37
  183.9 3.4 copy.98
  187.3 4.8 %bitcast_reduce_fusion.1 = (f32[64,32]{0,1:T(8,128)S(1)}, f32[128,32,64]{2,1,0:T(8,128)S(1)}) fusion(bf16[32,256,128]{1,0,2:T(8,128)(2,1)S(1)} %copy.98, bf16[64,256,128]{0,1,2:T(8,128)(2,1)} %copy.99), kind=kOutput, calls=%fused_computation.9 | convolution fusion | flops 134477824 | bytes 7348224 | tf_op jit(solution)/shard_map/ikc,jkc->ijc/dot_general | solution.py:102
  192.1 0.3 multiply_reduce_fusion.1
  192.5 0.4 add_convert_fusion.1
  192.9 1.5 copy.102
  194.4 1.8 convert_reduce_fusion
  196.3 0.1 copy.105
  196.4 0.6 fusion.10
  197.1 0.1 copy.107
  197.2 1.0 fusion.48
  198.2 1.8 fusion.19
  200.0 0.7 copy-done.1
  200.7 0.2 all-reduce.6.cloned.1.call-start
  201.0 0.5 collective-permute-start
  201.4 47.0 %all-gather.8.cloned.1.call-done = bf16[256,32,128]{2,1,0:T(8,128)(2,1)} async-done(((bf16[64,32,128]{2,1,0:T(8,128)(2,1)}), bf16[256,32,128]{2,1,0:T(8,128)(2,1)}) %all-gather.8.cloned.1.call-update) | async-done | bytes 2097168 | tf_op jit(solution)/shard_map/all_gather | solution.py:112
  248.4 3.9 %copy.111 = bf16[256,32,128]{0,1,2:T(8,128)(2,1)S(1)} copy(bf16[256,32,128]{2,1,0:T(8,128)(2,1)} %all-gather.8.cloned.1.call-done) | data formatting | bytes 4194304 | tf_op jit(solution)/shard_map/all_gather | solution.py:112
  252.4 2.3 broadcast_select_fusion.1
  254.7 1.1 pad_maximum_fusion.1
  255.9 0.4 fusion.45
  256.3 2.1 collective-permute-start.1
  258.4 0.1 copy.129
  258.5 0.1 copy.115
  258.7 0.1 reshape.154
  258.8 45.9 %collective-permute-done.1 = bf16[2,64,32,128]{3,2,1,0:T(8,128)(2,1)} collective-permute-done((bf16[2,64,32,128]{3,2,1,0:T(8,128)(2,1)S(1)}, bf16[2,64,32,128]{3,2,1,0:T(8,128)(2,1)}, u32[]{:S(2)}, u32[]{:S(2)}) %collective-permute-start.1) | collective-permute-done | bytes 1048608 | tf_op jit(solution)/shard_map/ppermute | solution.py:21
  304.7 1.4 pad_maximum_fusion
  306.1 0.5 reverse_select_fusion
  306.6 3.6 %copy.113 = bf16[256,32,128]{0,1,2:T(8,128)(2,1)} copy(bf16[256,32,128]{2,1,0:T(8,128)(2,1)S(1)} %bitcast.94) | data formatting | bytes 4194304 | tf_op jit(solution)/shard_map/reshape;reshape | solution.py:12
  310.2 25.1 %all-reduce.6.cloned.1.call-done = (bf16[256,32,128]{0,1,2:T(8,128)(2,1)}, bf16[256,32,128]{0,1,2:T(8,128)(2,1)}) async-done(((bf16[256,32,128]{0,1,2:T(8,128)(2,1)}, bf16[256,32,128]{0,1,2:T(8,128)(2,1)}), (bf16[256,32,128]{0,1,2:T(8,128)(2,1)}, bf16[256,32,128]{0,1,2:T(8,128)(2,1)})) %all-reduce.6.cloned.1.call-update) | async-done | bytes 4194320 | tf_op jit(solution)/shard_map/psum | solution.py:37
  335.2 4.1 %bitcast_reduce_fusion = (f32[64,32]{0,1:T(8,128)S(1)}, f32[128,32,64]{2,1,0:T(8,128)S(1)}) fusion(bf16[256,32,128]{0,1,2:T(8,128)(2,1)} %copy.113, bf16[256,32,128]{0,1,2:T(8,128)(2,1)} %get-tuple-element.5, bf16[256,32,128]{0,1,2:T(8,128)(2,1)} %get-tuple-element.6), kind=kOutput, calls=%fused_computation.7 | convolution fusion | flops 142866432 | bytes 7348224 | tf_op jit(solution)/shard_map/kic,kjc->ijc/dot_general | solution.py:118
  339.3 0.3 multiply_reduce_fusion
  339.6 0.4 add_convert_fusion
  340.1 1.5 copy.116
  341.6 2.4 fusion.5
  (41 shorter events, 0.8 us)
Async XLA Ops:
  6.5 4.6 %copy-start.2 = (bf16[64,32,128]{2,1,0:T(8,128)(2,1)S(1)}, bf16[64,32,128]{2,1,0:T(8,128)(2,1)}, u32[]{:S(2)}) copy-start(bf16[64,32,128]{2,1,0:T(8,128)(2,1)} %param.8) | copy-start | bytes 1572868
  6.5 5.5 %copy-start.6 = (f32[2,2,128]{2,1,0:T(2,128)S(1)}, f32[2,2,128]{2,1,0:T(2,128)}, u32[]{:S(2)}) copy-start(f32[2,2,128]{2,1,0:T(2,128)} %param.10) | copy-start | bytes 6148
  6.5 5.5 %copy-start.5 = (f32[2,2,128]{2,1,0:T(2,128)S(1)}, f32[2,2,128]{2,1,0:T(2,128)}, u32[]{:S(2)}) copy-start(f32[2,2,128]{2,1,0:T(2,128)} %param.11) | copy-start | bytes 6148
  6.5 49.6 %all-gather.4.cloned.1.call-start = ((), (), s32[]{:S(2)}) async-start(), calls=%async_computation | async-start | bytes 4718592 | tf_op jit(solution)/shard_map/all_gather | solution.py:98
  13.2 2.7 copy-start
  15.9 79.5 %all-gather.6.cloned.1.call-start = ((), (), s32[]{:S(2)}) async-start(), calls=%async_computation.2 | async-start | bytes 4718592 | tf_op jit(solution)/shard_map/all_gather | solution.py:104
  16.6 167.3 %all-reduce.4.cloned.1.call-start = ((), (), s32[]{:S(2)}) async-start(), calls=%async_computation.1 | async-start | bytes 4194304 | tf_op jit(solution)/shard_map/psum | solution.py:37
  59.2 0.8 copy-start.3
  59.2 1.0 copy-start.4
  59.2 189.2 %all-gather.8.cloned.1.call-start = ((), (), s32[]{:S(2)}) async-start(), calls=%async_computation.3 | async-start | bytes 2621440 | tf_op jit(solution)/shard_map/all_gather | solution.py:112
  198.2 2.5 copy-start.1
  200.7 134.5 %all-reduce.6.cloned.1.call-start = ((), (), s32[]{:S(2)}) async-start(), calls=%async_computation.4 | async-start | bytes 8388608 | tf_op jit(solution)/shard_map/psum | solution.py:37
  201.0 53.8 %collective-permute-start = (bf16[1,64,32,128]{3,2,1,0:T(8,128)(2,1)S(1)}, bf16[1,64,32,128]{3,2,1,0:T(8,128)(2,1)}, u32[]{:S(2)}, u32[]{:S(2)}) collective-permute-start(bf16[1,64,32,128]{3,2,1,0:T(8,128)(2,1)S(1)} %bitcast.95), channel_id=1, source_target_pairs={{0,8},{8,0},{16,24},{24,16},{1,9},{9,1},{17,25},{25,17},{2,10},{10... | collective-permute-start | bytes 1572872 | tf_op jit(solution)/shard_map/ppermute | solution.py:21
  256.3 48.4 %collective-permute-start.1 = (bf16[2,64,32,128]{3,2,1,0:T(8,128)(2,1)S(1)}, bf16[2,64,32,128]{3,2,1,0:T(8,128)(2,1)}, u32[]{:S(2)}, u32[]{:S(2)}) collective-permute-start(bf16[2,64,32,128]{3,2,1,0:T(8,128)(2,1)S(1)} %get-tuple-element.14), channel_id=1, source_target_pairs={{0,16},{8,24},{16,0},{24,8},{1,17},{9,25},{17,1},{25,9},{2,18},{10... | collective-permute-start | bytes 3145736 | tf_op jit(solution)/shard_map/ppermute | solution.py:21
Sparse Core Ops, SparseCore 0:
  16.0 40.0 all-gather.3
  58.0 37.3 all-gather.5
  97.7 86.1 all-reduce.3
  200.9 47.5 all-gather.7
  254.8 80.3 all-reduce.5
